TPU v7x, 512 devices: a whole 4x4x16 slice. The times are simulated.
512 devices in a mesh: ctx: 64 (over y, z), exp: 8 (over x, core).
Axes of the slice: x: 4, y: 4, z: 16, core: 2. Of those that a mesh axis runs over, the one named last changes fastest.
Arguments:
- ssm_input: bfloat16 [8192, 4096], P('ctx', 'exp'), may hold values from -6 to 6
- gate_input: bfloat16 [8192, 4096], P('ctx', 'exp'), may hold values from -6 to 6
- b_input: bfloat16 [8192, 1024], P('ctx', 'exp'), may hold values from -6 to 6
- c_input: bfloat16 [8192, 1024], P('ctx', 'exp'), may hold values from -6 to 6
- step_size: float32 [64, 8192], P('exp', 'ctx'), may hold values from 0.5 to 16384
- decay_rate: float32 [64], P('exp'), may hold values from 2.4414063e-05 to 0.1
- norm_gain: float32 [4096], P('exp'), may hold values from 0.1 to 1.9
- out_weight: bfloat16 [4096, 2048], P('exp'), may hold values from -0.125 to 0.125
- stream: bfloat16 [8192, 2048], P('ctx', 'exp'), may hold values from -7 to 7
- moe_gain: float32 [2048], replicated, may hold values from 0.1 to 1.9
- router: bfloat16 [2048, 64], replicated, may hold values from -0.125 to 0.125
- expert_ids: int32 [8192, 6], P('ctx'), may hold values from 0 to 63, all different within a row; in each aligned block of 128 rows (0 to 127, 128 to 255, ...) at most 15 rows name the same one
- w_gate: bfloat16 [64, 1408, 2048], P('ctx', 'exp'), may hold values from -0.125 to 0.125
- w_up: bfloat16 [64, 1408, 2048], P('ctx', 'exp'), may hold values from -0.125 to 0.125
- w_down: bfloat16 [64, 1408, 2048], P('ctx', 'exp'), may hold values from -0.21875 to 0.21875
Outputs:
- layer_out: bfloat16 [8192, 2048], P('ctx', 'exp')
Inputs may be any that keep to these rules, and one draw needn't show every extreme that they name: `expert_ids`: each row names 6 different experts; among the 128 rows of one device (aligned blocks of 128 rows) no expert is named by more than 15 rows, a bound that some block reaches.
All inputs are finite; a program needn't handle non-finite values.
Results may differ from a plain program's by a relative error of at most 0.024.
Values may be sent and summed in bfloat16 or wider, within the bound.
A program may use at most 64 MiB of HBM per device.

v0:
```python
import jax
import jax.numpy as jnp
from jax import lax
from jax.sharding import PartitionSpec as P

P_SIZE = 64
N = 128


def entering_2(part, axis, combine, identity):
    place = lax.axis_index(axis)
    gathered = jax.tree.map(lambda a: lax.all_gather(a, axis), part)
    state = jax.tree.map(lambda a, e: jnp.zeros_like(a) + jnp.asarray(e, a.dtype), part, identity)

    def one(step, state):
        return combine(
            state, jax.tree.map(lambda a: lax.dynamic_index_in_dim(a, step, 0, False), gathered)
        )

    return lax.fori_loop(0, place, one, state)


def chain_combine(earlier, later):
    return (earlier[0] * later[0], later[0][:, :, None, None] * earlier[1] + later[1])


def run_rows(pieces, w_gate, w_up, w_down):
    row_count = pieces.shape[0] * pieces.shape[1]
    flattened = pieces.reshape(row_count, pieces.shape[2])
    contract = (((1,), (1,)), ((), ()))
    gate_proj = lax.dot_general(flattened, w_gate[0], contract, preferred_element_type=jnp.float32)
    up_proj = lax.dot_general(flattened, w_up[0], contract, preferred_element_type=jnp.float32)
    active = (jax.nn.silu(gate_proj) * up_proj).astype(jnp.bfloat16)
    partial_value = jnp.dot(active, w_down[0], preferred_element_type=jnp.float32).astype(
        jnp.bfloat16
    )
    full_width = partial_value.shape[1]
    shaped = partial_value.reshape(pieces.shape[0], pieces.shape[1], full_width)
    return lax.all_to_all(shaped, "ctx", split_axis=0, concat_axis=0, tiled=True)


def per_device(
    ssm_input,
    gate_input,
    b_input,
    c_input,
    step_size,
    decay_rate,
    norm_gain,
    out_weight,
    stream,
    moe_gain,
    router,
    expert_ids,
    w_gate,
    w_up,
    w_down,
):
    token_count = ssm_input.shape[0]
    head_count = step_size.shape[0]
    group_count = b_input.shape[1] // N
    per_group = head_count // group_count
    log_decay = -step_size * decay_rate[:, None]
    running = jnp.cumsum(log_decay, axis=1).T.reshape(token_count, group_count, per_group)
    shaped_x = ssm_input.reshape(token_count, group_count, per_group, P_SIZE)
    step_rows = step_size.T.reshape(token_count, group_count, per_group)
    weighted = (step_rows[..., None] * shaped_x).astype(jnp.bfloat16)
    b_block = b_input.reshape(token_count, group_count, N)
    c_block = c_input.reshape(token_count, group_count, N)
    scores = jnp.einsum("tgn,sgn->gts", c_block, b_block, preferred_element_type=jnp.float32)
    ordered = running.transpose(1, 2, 0)
    spread = ordered[:, :, :, None] - ordered[:, :, None, :]
    lower_mask = jnp.arange(token_count)[:, None] >= jnp.arange(token_count)[None, :]
    decay_mat = jnp.where(lower_mask, jnp.exp(jnp.where(lower_mask, spread, 0.0)), 0.0)
    mixing = (decay_mat * scores[:, None]).astype(jnp.bfloat16)
    inner = jnp.einsum("gqts,sgqp->tgqp", mixing, weighted, preferred_element_type=jnp.float32)
    tail_decay = jnp.exp(running[-1:] - running)
    carried = (tail_decay[..., None] * weighted).astype(jnp.bfloat16)
    block_state = jnp.einsum("tgqp,tgn->gqpn", carried, b_block, preferred_element_type=jnp.float32)
    block_decay = jnp.exp(running[-1])
    identity = (jnp.ones_like(block_decay), jnp.zeros_like(block_state))
    entry_decay, entering = entering_2((block_decay, block_state), "ctx", chain_combine, identity)
    carried_in = jnp.einsum(
        "tgn,gqpn->tgqp", c_block.astype(jnp.float32), entering, precision=lax.Precision.HIGHEST
    )
    ssd_out = (inner + jnp.exp(running)[..., None] * carried_in).reshape(
        token_count, group_count, per_group * P_SIZE
    )
    gated = ssd_out * jax.nn.silu(gate_input.astype(jnp.float32)).reshape(
        token_count, group_count, per_group * P_SIZE
    )
    mean_sq = jnp.mean(gated * gated, axis=-1, keepdims=True)
    normed = (
        (gated * lax.rsqrt(mean_sq + 1e-05)).reshape(token_count, head_count * P_SIZE) * norm_gain
    ).astype(jnp.bfloat16)
    mixer = jnp.dot(normed, out_weight, preferred_element_type=jnp.float32)
    slice_width = stream.shape[1]
    start_col = lax.axis_index("exp") * slice_width
    expert_count = router.shape[1]
    top_count = expert_ids.shape[1]
    capacity = max(
        2, token_count * top_count // expert_count + token_count * top_count // (4 * expert_count)
    )
    own_cols = lax.dynamic_slice_in_dim(mixer, start_col, slice_width, 1) + stream.astype(
        jnp.float32
    )
    with_stream = lax.dynamic_update_slice_in_dim(mixer, own_cols, start_col, 1)
    hidden_all = lax.psum(with_stream.astype(jnp.bfloat16), "exp")
    hidden_own = lax.dynamic_slice_in_dim(hidden_all, start_col, slice_width, 1)
    hidden_f = hidden_all.astype(jnp.float32)
    mean_h = jnp.mean(hidden_f * hidden_f, axis=1, keepdims=True)
    sent_rows = (hidden_f * lax.rsqrt(mean_h + 1e-06) * moe_gain).astype(jnp.bfloat16)
    logits = jnp.dot(sent_rows, router, preferred_element_type=jnp.float32)
    sigmoid_score = jax.nn.sigmoid(logits)
    expert_range = jnp.arange(expert_count, dtype=jnp.int32)
    matches = expert_ids[:, :, None] == expert_range
    picked = jnp.sum(jnp.where(matches, sigmoid_score[:, None, :], 0.0), axis=2)
    gates = picked / jnp.sum(picked, axis=1, keepdims=True)
    flat_ids = expert_ids.reshape(-1)
    one_hot = (flat_ids[:, None] == expert_range).astype(jnp.int32)
    slot_index = jnp.sum((jnp.cumsum(one_hot, axis=0) - one_hot) * one_hot, axis=1)
    target = flat_ids * capacity + slot_index
    token_of = jnp.arange(token_count * top_count, dtype=jnp.int32) // top_count
    source_row = (
        jnp.full((expert_count * capacity,), token_count, jnp.int32).at[target].set(token_of)
    )
    padded = jnp.concatenate([sent_rows, jnp.zeros((1, sent_rows.shape[1]), jnp.bfloat16)], axis=0)
    outgoing = padded[source_row].reshape(expert_count, capacity, sent_rows.shape[1])
    returned = run_rows(
        lax.all_to_all(outgoing, "ctx", split_axis=0, concat_axis=0, tiled=True),
        w_gate,
        w_up,
        w_down,
    )
    back_width = returned.shape[2]
    flat_back = returned.reshape(expert_count * capacity, back_width)
    slot_rows = target.reshape(token_count, top_count)
    moe_part = jnp.zeros((token_count, back_width), jnp.float32)
    for choice_number in range(top_count):
        picked_rows = flat_back[slot_rows[:, choice_number]].astype(jnp.float32)
        moe_part = moe_part + gates[:, choice_number][:, None] * picked_rows
    moe_sum = lax.psum_scatter(
        moe_part.astype(jnp.bfloat16), "exp", scatter_dimension=1, tiled=True
    ).astype(jnp.float32)
    return (hidden_own.astype(jnp.float32) + moe_sum).astype(jnp.bfloat16)


def solution(mesh):
    in_specs = (
        P("ctx", "exp"),
        P("ctx", "exp"),
        P("ctx", "exp"),
        P("ctx", "exp"),
        P("exp", "ctx"),
        P("exp"),
        P("exp"),
        P("exp", None),
        P("ctx", "exp"),
        P(),
        P(),
        P("ctx", None),
        P("ctx", "exp", None),
        P("ctx", "exp", None),
        P("ctx", "exp", None),
    )
    out_specs = P("ctx", "exp")
    return jax.shard_map(
        per_device, mesh=mesh, in_specs=in_specs, out_specs=out_specs, check_vma=False
    )
```

profile of v0, /device:TPU:1, one launch (start us, length us, event | category | flops | bytes accessed | tf_op | source)
XLA Modules:
  0.0 856.3 jit_solution(5610821369075495253)
XLA Ops:
  9.8 1.6 fusion.47
  12.7 1.8 reduce-window.6
  15.2 3.4 scatter_custom_fusion
  18.6 72.3 %all-gather.2 = f32[64,1,8]{2,1,0:T(1,128)S(1)} all-gather(f32[1,1,8]{2,1,0:T(1,128)S(1)} %bitcast.109), channel_id=2, replica_groups=mesh['ctx'=64,'exp'=8] {'ctx'}, dimensions={0}, use_global_device_ids=true | all-gather | bytes 2080 | tf_op jit(solution)/shard_map/all_gather | solution.py:12
  91.8 118.3 %all-gather.5.cloned.1.call-done = f32[512,64,128]{2,1,0:T(8,128)} async-done(((f32[8,64,128]{2,1,0:T(8,128)}), f32[512,64,128]{2,1,0:T(8,128)}) %all-gather.5.cloned.1.call-update) | async-done | bytes 16777232 | tf_op jit(solution)/shard_map/all_gather | solution.py:12
  212.6 134.8 %all-reduce.3.cloned.1.call-done = bf16[128,2048]{1,0:T(8,128)(2,1)} async-done(((bf16[128,2048]{1,0:T(8,128)(2,1)}), bf16[128,2048]{1,0:T(8,128)(2,1)}) %all-reduce.3.cloned.1.call-update) | async-done | bytes 524304 | tf_op jit(solution)/shard_map/psum | solution.py:108
  350.0 5.9 gather_fusion
  355.9 5.1 reshape.180
  361.0 196.4 %all_to_all.10 = bf16[64,15,2048]{2,1,0:T(8,128)(2,1)} all-to-all(bf16[64,15,2048]{2,1,0:T(8,128)(2,1)} %reshape.180), channel_id=1, replica_groups=mesh['ctx'=64,'exp'=8] {'ctx'}, dimensions={0} | all-to-all | bytes 7864320 | tf_op jit(solution)/shard_map/all_to_all | solution.py:130
  557.5 5.1 reshape.181
  562.6 4.5 fusion.12
  567.1 7.1 convolution_convert_fusion
  574.2 5.1 reshape.182
  579.3 12.9 %all-to-all-start.1 = ((bf16[64,15,2048]{2,1,0:T(8,128)(2,1)}), bf16[64,15,2048]{2,1,0:T(8,128)(2,1)}, u32[]{:S(2)}, u32[]{:S(2)}) async-start(bf16[64,15,2048]{2,1,0:T(8,128)(2,1)} %reshape.182), calls=%async_computation.1 | async-start | bytes 8388608 | tf_op jit(solution)/shard_map/all_to_all | solution.py:39
  593.2 179.5 %all-to-all-done.1 = bf16[64,15,2048]{2,1,0:T(8,128)(2,1)} async-done(((bf16[64,15,2048]{2,1,0:T(8,128)(2,1)}), bf16[64,15,2048]{2,1,0:T(8,128)(2,1)}, u32[]{:S(2)}, u32[]{:S(2)}) %all-to-all-start.1) | async-done | bytes 3932192 | tf_op jit(solution)/shard_map/all_to_all | solution.py:39
  772.7 5.1 reshape.183
  777.8 4.1 gather_fusion.1
  781.9 4.1 gather_fusion.2
  786.0 4.9 gather_fusion.3
  790.9 4.9 gather_fusion.4
  795.7 4.8 gather_fusion.5
  800.6 4.9 gather_fusion.6
  805.4 3.0 add_convert_fusion
  808.5 39.8 %reduce-scatter.2.cloned.1.call-done = bf16[128,256]{1,0:T(8,128)(2,1)} async-done(((bf16[128,2048]{1,0:T(8,128)(2,1)}), bf16[128,256]{1,0:T(8,128)(2,1)}) %reduce-scatter.2.cloned.1.call-update) | async-done | bytes 65552 | tf_op jit(solution)/shard_map/reduce_scatter | solution.py:142
  (69 shorter events, 13.5 us)
Async XLA Ops:
  6.5 204.6 %copy-start = (bf16[512,2048]{1,0:T(8,128)(2,1)S(1)}, bf16[512,2048]{1,0:T(8,128)(2,1)}, u32[]{:S(2)}) copy-start(bf16[512,2048]{1,0:T(8,128)(2,1)} %param.24) | copy-start | bytes 6291460
  6.5 203.6 %copy-start.3 = (bf16[128,128]{1,0:T(8,128)(2,1)S(1)}, bf16[128,128]{1,0:T(8,128)(2,1)}, u32[]{:S(2)}) copy-start(bf16[128,128]{1,0:T(8,128)(2,1)} %param.20) | copy-start | bytes 98308
  6.5 203.6 %all-gather.5.cloned.1.call-start = ((), (), s32[]{:S(2)}) async-start(), calls=%async_computation.5 | async-start | bytes 17039360 | tf_op jit(solution)/shard_map/all_gather | solution.py:12
  9.0 201.4 %copy-start.5 = (f32[8,128]{1,0:T(8,128)S(1)}, f32[8,128]{1,0:T(8,128)}, u32[]{:S(2)}) copy-start(f32[8,128]{1,0:T(8,128)} %param.21) | copy-start | bytes 12292
  11.5 336.0 %all-reduce.3.cloned.1.call-start = ((), (), s32[]{:S(2)}) async-start(), calls=%async_computation.3 | async-start | bytes 1048576 | tf_op jit(solution)/shard_map/psum | solution.py:108
  14.5 196.5 %copy-start.1 = (bf16[128,512]{1,0:T(8,128)(2,1)S(1)}, bf16[128,512]{1,0:T(8,128)(2,1)}, u32[]{:S(2)}) copy-start(bf16[128,512]{1,0:T(8,128)(2,1)} %param.18) | copy-start | bytes 393220
  14.8 196.4 %copy-start.8 = (f32[512]{0:T(512)S(1)}, f32[512]{0:T(512)}, u32[]{:S(2)}) copy-start(f32[512]{0:T(512)} %param.23) | copy-start | bytes 6148
  210.2 1.5 copy-start.4
  210.8 137.9 %copy-start.7 = (f32[2048]{0:T(1024)S(1)}, f32[2048]{0:T(1024)}, u32[]{:S(2)}) copy-start(f32[2048]{0:T(1024)} %param.26) | copy-start | bytes 24580
  579.3 13.5 %copy-start.2 = (bf16[2048,64]{0,1:T(8,128)(2,1)S(1)}, bf16[2048,64]{0,1:T(8,128)(2,1)}, u32[]{:S(2)}) copy-start(bf16[2048,64]{0,1:T(8,128)(2,1)} %param.27) | copy-start | bytes 786436
  579.3 13.8 %copy-start.6 = (s32[128,6]{0,1:T(8,128)S(1)}, s32[128,6]{0,1:T(8,128)}, u32[]{:S(2)}) copy-start(s32[128,6]{0,1:T(8,128)} %param.28) | copy-start | bytes 9220
  579.3 193.5 %all-to-all-start.1 = ((bf16[64,15,2048]{2,1,0:T(8,128)(2,1)}), bf16[64,15,2048]{2,1,0:T(8,128)(2,1)}, u32[]{:S(2)}, u32[]{:S(2)}) async-start(bf16[64,15,2048]{2,1,0:T(8,128)(2,1)} %reshape.182), calls=%async_computation.1 | async-start | bytes 8388608 | tf_op jit(solution)/shard_map/all_to_all | solution.py:39
  592.2 256.1 %reduce-scatter.2.cloned.1.call-start = ((), (), s32[]{:S(2)}) async-start(), calls=%async_computation.4 | async-start | bytes 589824 | tf_op jit(solution)/shard_map/reduce_scatter | solution.py:142
Sparse Core Ops, SparseCore 0:
  11.6 198.4 all-gather.4
  212.7 134.6 all-reduce.2
  808.6 39.6 reduce-scatter.1
where the time goes:
time: 860 us; the launch traced here: 856 us
  waiting for transfers between devices  473 us (55%)
  blocking collectives  269 us (31%)
  local copies, waits for them, and re-layouts  60.4 us (7%)
  matrix products  15.6 us (2%)
  between operations  13.4 us (2%)
  starting transfers between devices  13.2 us (2%)
  other arithmetic  12.5 us (1%)
    all_to_all x1, blocking collectives, per_device(): lax.all_to_all(outgoing, 'ctx', split_axis=0, concat_axis=0, tiled=True)  196 us
    all_to_all x1, waiting for transfers between devices, run_rows(): lax.all_to_all(shaped, 'ctx', split_axis=0, concat_axis=0, tiled=True)  180 us
    psum x1, waiting for transfers between devices, per_device(): hidden_all = lax.psum(with_stream.astype(jnp.bfloat16), 'exp')  135 us
    all_gather x1, waiting for transfers between devices, entering_2(): gathered = jax.tree.map(lambda a: lax.all_gather(a, axis), part)  118 us
    all_gather x1, blocking collectives, entering_2(): gathered = jax.tree.map(lambda a: lax.all_gather(a, axis), part)  72.3 us
    reduce_scatter x1, waiting for transfers between devices, per_device(): lax.psum_scatter(moe_part.astype(jnp.bfloat16), 'exp', scatter_dimension=...  39.8 us
    gather x6, local copies, waits for them, and re-layouts, per_device(): picked_rows = flat_back[slot_rows[:, choice_number]].astype(jnp.float32)  27.6 us
  transfers between devices with their start and end apart: 4, of which 4 were waited for; matrix products, arithmetic and copies ran while one was open for 1% of the time, Pallas kernels for 0%

commit v1 on v0

v1 whole, which is shorter than its diff:
```python
import functools

import jax
import jax.numpy as jnp
from jax import lax
from jax.experimental import pallas as pl
from jax.experimental.pallas import tpu as pltpu
from jax.sharding import PartitionSpec as P

P_SIZE = 64
N = 128
LANES = 128
SLOTS = 16
CORES = 2
MESH = pl.DeviceIdType.MESH
NT = (((1,), (1,)), ((), ()))
f32 = jnp.float32
bf16 = jnp.bfloat16


def iota(shape, dim):
    return lax.broadcasted_iota(jnp.int32, shape, dim)


def dot(a, b):
    return jnp.dot(a, b, preferred_element_type=f32)


def silu(v):
    return v / (1.0 + jnp.exp(-v))


def leading(v):
    scaled = v * 65537.0
    return scaled - (scaled - v)


def wait_bytes(ref, count, sem):
    view = ref.at[pl.ds(0, count)]
    pltpu.make_async_copy(view, view, sem).wait()


def layer_kernel(
    n_ctx,
    n_exp,
    x_ref,
    z_ref,
    b_ref,
    c_ref,
    step_ref,
    rate_ref,
    norm_gain_ref,
    out_w_hbm,
    stream_ref,
    moe_gain_ref,
    router_ref,
    ids_ref,
    w_gate_hbm,
    w_up_hbm,
    w_down_hbm,
    out_ref,
    out_w,
    w_gate,
    w_up,
    w_down,
    state_out,
    state_in,
    enter_out,
    enter_in,
    inner,
    mixed,
    mix_out,
    mix_in,
    hidden,
    expert_in,
    rows_f32,
    rows_out,
    rows_in,
    tokens,
    act,
    back_out,
    back_in,
    moe_out,
    moe_in,
    local_sem,
    ctx_send,
    ctx_recv,
    exp_send,
    exp_recv,
    w_send,
    w_recv,
):
    me_c, me_e = lax.axis_index("ctx"), lax.axis_index("exp")
    token_count, width = x_ref.shape
    head_count = step_ref.shape[0]
    pair_count = width // LANES
    part_rows = width // n_ctx
    cols = stream_ref.shape[1]
    d_model = cols * n_exp
    ff_part = w_gate_hbm.shape[0]
    ff_total = ff_part * n_exp
    per_dev = SLOTS // n_exp
    row_count = n_ctx * per_dev
    stride = per_dev * n_exp

    def ctx_peer(d):
        return lax.rem(me_c + d, n_ctx)

    def exp_peer(d):
        return lax.rem(me_e + d, n_exp)

    def to_exp(src, dst, send, recv, peer):
        return pltpu.make_async_remote_copy(
            src_ref=src,
            dst_ref=dst,
            send_sem=send,
            recv_sem=recv,
            device_id=(me_c, peer),
            device_id_type=MESH,
        )

    def exchange(src, dst, phase):
        def one(d, carry):
            peer = ctx_peer(d)
            pltpu.make_async_remote_copy(
                src_ref=src.at[peer],
                dst_ref=dst.at[me_c],
                send_sem=ctx_send.at[phase],
                recv_sem=ctx_recv.at[phase],
                device_id=(peer, me_e),
                device_id_type=MESH,
            ).start()
            return carry

        lax.fori_loop(1, n_ctx, one, 0)

    barrier = pltpu.get_barrier_semaphore()

    def greet_ctx(d, carry):
        pl.semaphore_signal(barrier, inc=1, device_id=(ctx_peer(d), me_e), device_id_type=MESH)
        return carry

    def greet_exp(d, carry):
        pl.semaphore_signal(barrier, inc=1, device_id=(me_c, exp_peer(d)), device_id_type=MESH)
        return carry

    lax.fori_loop(1, n_ctx, greet_ctx, 0)
    lax.fori_loop(1, n_exp, greet_exp, 0)

    out_w_copy = pltpu.make_async_copy(out_w_hbm, out_w, local_sem.at[0])
    out_w_copy.start()
    weights = ((w_gate_hbm, w_gate), (w_up_hbm, w_up), (w_down_hbm, w_down))

    def part(ref, index, first=0, rows=ff_part):
        return ref.at[pl.ds(pl.multiple_of(index * ff_part + first, 16), rows)]

    own_copies = [
        pltpu.make_async_copy(hbm, part(buf, me_e), local_sem.at[1 + i])
        for i, (hbm, buf) in enumerate(weights)
    ]
    for copy in own_copies:
        copy.start()

    step = step_ref[...]
    lane_t = iota((head_count, token_count), 1)
    running = -(step * rate_ref[...])
    shift = 1
    while shift < token_count:
        running = running + jnp.where(lane_t >= shift, pltpu.roll(running, shift, 1), 0.0)
        shift *= 2
    stacked = jnp.concatenate(
        [running, step, jnp.zeros((token_count - 2 * head_count, token_count), f32)], axis=0
    )
    by_token = stacked.T
    run_t = by_token[:, 0:head_count]
    step_t = by_token[:, head_count : 2 * head_count]
    last = run_t[token_count - 1 : token_count, :]
    tail = jnp.exp(last - run_t)
    grown = jnp.exp(run_t)
    total_decay = jnp.exp(last)

    first_half = iota((token_count, LANES), 1) < P_SIZE

    def expand(per_head, k):
        return jnp.where(
            first_half, per_head[:, 2 * k : 2 * k + 1], per_head[:, 2 * k + 1 : 2 * k + 2]
        )

    b_block, c_block = b_ref[...], c_ref[...]
    scores = lax.dot_general(c_block, b_block, NT, preferred_element_type=f32)
    lower = iota((token_count, token_count), 0) >= iota((token_count, token_count), 1)

    def mix_head(h, weighted):
        spread = run_t[:, h : h + 1] - running[h : h + 1, :]
        decay = jnp.where(lower, jnp.exp(jnp.where(lower, spread, 0.0)), 0.0)
        return dot((decay * scores).astype(bf16), weighted)

    row8 = iota((8, N), 0)
    for k in range(pair_count):
        lanes = slice(k * LANES, (k + 1) * LANES)
        weighted = (expand(step_t, k) * x_ref[:, lanes].astype(f32)).astype(bf16)
        inner[:, lanes] = jnp.where(
            first_half, mix_head(2 * k, weighted), mix_head(2 * k + 1, weighted)
        )
        carried = (expand(tail, k) * weighted.astype(f32)).T.astype(bf16)
        state = dot(carried, b_block)
        for i in range(LANES // part_rows):
            j = k * LANES // part_rows + i
            head = j * part_rows // P_SIZE
            decay = jnp.broadcast_to(total_decay[:, head : head + 1], (8, N))
            high = leading(decay)
            middle = leading(decay - high)
            low = decay - high - middle
            decay_rows = jnp.where(
                row8 == 0, high, jnp.where(row8 == 1, middle, jnp.where(row8 == 2, low, 0.0))
            )
            piece = state[i * part_rows : (i + 1) * part_rows, :]
            lead = leading(piece)
            state_out[j] = jnp.concatenate([lead, piece - lead, decay_rows], axis=0).astype(bf16)

    pl.semaphore_wait(barrier, n_ctx - 1 + n_exp - 1)

    exchange(state_out, state_in, 0)

    chips = n_exp // CORES
    me_x, core = me_e // CORES, lax.rem(me_e, CORES)

    def at_chip(d):
        return lax.rem(me_x + d, chips) * CORES + core

    right, left, opposite = at_chip(1), at_chip(chips - 1), at_chip(2)
    sibling = me_x * CORES + 1 - core
    half = ff_part // 32 * 16

    def send_part(buf, index, first, rows, group, arrival, peer, hbm=None):
        to_exp(
            part(buf, index, first, rows) if hbm is None else hbm,
            part(buf, index, first, rows),
            w_send.at[group],
            w_recv.at[arrival],
            peer,
        ).start()

    for hbm, buf in weights:
        send_part(buf, me_e, 0, ff_part, 0, 0, right, hbm)
        send_part(buf, me_e, 0, ff_part, 0, 1, left, hbm)
    for hbm, buf in weights:
        send_part(buf, me_e, 0, ff_part, 1, 3, sibling, hbm)

    def pass_on_neighbours():
        wait_bytes(w_gate, 3 * ff_part, w_recv.at[0])
        wait_bytes(w_gate, 3 * ff_part, w_recv.at[1])
        for _, buf in weights:
            send_part(buf, left, 0, half, 2, 2, right)
            send_part(buf, right, half, ff_part - half, 2, 2, left)
        for _, buf in weights:
            send_part(buf, left, 0, ff_part, 3, 4, sibling)
            send_part(buf, right, 0, ff_part, 3, 4, sibling)

    def pass_on_opposite():
        wait_bytes(w_gate, 3 * ff_part, w_recv.at[2])
        for _, buf in weights:
            send_part(buf, opposite, 0, ff_part, 4, 5, sibling)

    state_in[me_c] = state_out[me_c]
    wait_bytes(state_in, n_ctx - 1, ctx_recv.at[0])

    def chain(i, entering):
        enter_out[i] = entering
        block = state_in[i].astype(f32)
        r = part_rows
        terms = block[2 * r : 2 * r + 8]
        decay = terms[0:1] + terms[1:2] + terms[2:3]
        return decay * entering + (block[0:r] + block[r : 2 * r])

    lax.fori_loop(0, n_ctx, chain, jnp.zeros((part_rows, N), f32))
    exchange(enter_out, enter_in, 1)
    enter_in[me_c] = enter_out[me_c]

    lane_r = iota((token_count, row_count), 1)
    expert_of, slot_of = lax.rem(lane_r, n_ctx), lane_r // n_ctx
    named = jnp.zeros((token_count, row_count), f32)
    for k in range(ids_ref.shape[1]):
        named = named + jnp.where(ids_ref[:, k : k + 1] == expert_of, 1.0, 0.0)
    strictly = iota((token_count, token_count), 0) > iota((token_count, token_count), 1)
    rank = dot(jnp.where(strictly, 1.0, 0.0).astype(bf16), named.astype(bf16))
    wanted = (slot_of + me_e * per_dev).astype(f32)
    chosen = jnp.where(rank == wanted, named, 0.0)
    rows_of = chosen.T.astype(bf16)
    gating = [silu(z_ref[:, k * LANES : (k + 1) * LANES].astype(f32)) for k in range(pair_count)]

    wait_bytes(enter_in, n_ctx - 1, ctx_recv.at[1])
    entering = enter_in[...].reshape(width, N)
    lead = leading(entering)
    carried_in = lax.dot_general(
        c_block, lead.astype(bf16), NT, preferred_element_type=f32
    ) + lax.dot_general(
        c_block, (entering - lead).astype(bf16), NT, preferred_element_type=f32
    )
    gated = []
    for k in range(pair_count):
        lanes = slice(k * LANES, (k + 1) * LANES)
        ssd_out = inner[:, lanes] + expand(grown, k) * carried_in[:, lanes]
        gated.append(ssd_out * gating[k])
    squares = gated[0] * gated[0]
    for g in gated[1:]:
        squares = squares + g * g
    inverse = lax.rsqrt(jnp.sum(squares, axis=1, keepdims=True) / width + 1e-05)
    for k in range(pair_count):
        lanes = slice(k * LANES, (k + 1) * LANES)
        mixed[:, lanes] = (gated[k] * inverse * norm_gain_ref[:, lanes]).astype(bf16)

    out_w_copy.wait()

    def out_columns(q):
        return dot(mixed[...], out_w[:, pl.ds(pl.multiple_of(q * cols, cols), cols)])

    for d in range(1, n_exp):
        peer = exp_peer(d)
        mix_out[peer] = out_columns(peer).astype(bf16)
        to_exp(mix_out.at[peer], mix_in.at[me_e], exp_send.at[0], exp_recv.at[0], peer).start()
    own = out_columns(me_e) + stream_ref[...].astype(f32)
    wait_bytes(mix_in, n_exp - 1, exp_recv.at[0])
    for d in range(1, n_exp):
        own = own + mix_in[exp_peer(d)].astype(f32)
    hidden[me_e] = own.astype(bf16)
    for d in range(1, n_exp):
        to_exp(
            hidden.at[me_e], hidden.at[me_e], exp_send.at[1], exp_recv.at[1], exp_peer(d)
        ).start()
    wait_bytes(mix_in, n_exp - 1, exp_recv.at[1])

    tiles = [slice(i * LANES, (i + 1) * LANES) for i in range(cols // LANES)]

    def spread_rows(q, value):
        for s in range(per_dev):
            for i, lanes in enumerate(tiles):
                rows_f32.at[i][pl.ds(s * n_exp + q, n_ctx, stride=stride), :] = value[
                    s * n_ctx : (s + 1) * n_ctx, lanes
                ]

    def pack(ref):
        for i, lanes in enumerate(tiles):
            ref[:, :, lanes] = rows_f32[i].reshape(n_ctx, stride, LANES).astype(bf16)

    def unpack(ref):
        for i, lanes in enumerate(tiles):
            rows_f32[i] = ref[:, :, lanes].astype(f32).reshape(n_ctx * stride, LANES)

    def column_rows(s, q):
        return jnp.concatenate(
            [
                rows_f32.at[i][pl.ds(s * n_exp + q, n_ctx, stride=stride), :]
                for i in range(len(tiles))
            ],
            axis=1,
        ).astype(bf16)

    squares = jnp.zeros((token_count, cols), f32)
    for q in range(n_exp):
        h = hidden[q].astype(f32)
        squares = squares + h * h
    inverse = lax.rsqrt(jnp.sum(squares, axis=1, keepdims=True) / d_model + 1e-06)
    for q in range(n_exp):
        columns = slice(q * cols, (q + 1) * cols)
        value = hidden[q].astype(f32) * inverse * moe_gain_ref[:, columns]
        expert_in[:, columns] = value.astype(bf16)
        spread_rows(q, dot(rows_of, expert_in[:, columns]))
    pack(rows_out)
    exchange(rows_out, rows_in, 2)
    rows_in[me_c] = rows_out[me_c]
    pass_on_neighbours()

    logits = dot(expert_in[...], router_ref[...])
    score = 1.0 / (1.0 + jnp.exp(-logits))
    picked_score = score * named[:, 0:n_ctx]
    gate = picked_score / jnp.sum(picked_score, axis=1, keepdims=True)
    gate_rows = jnp.concatenate([gate] * per_dev, axis=1) * chosen
    gate_lead = leading(gate_rows)
    gate_high = gate_lead.astype(bf16)
    gate_low = (gate_rows - gate_lead).astype(bf16)
    pass_on_opposite()

    wait_bytes(rows_in, n_ctx - 1, ctx_recv.at[2])

    unpack(rows_in)
    for q in range(n_exp):
        for s in range(per_dev):
            tokens[s * n_ctx : (s + 1) * n_ctx, q * cols : (q + 1) * cols] = column_rows(s, q)

    for copy in own_copies:
        copy.wait()
    wait_bytes(w_gate, 3 * ff_part, w_recv.at[3])
    wait_bytes(w_gate, 6 * ff_part, w_recv.at[4])
    wait_bytes(w_gate, 3 * ff_part, w_recv.at[5])

    def hidden_units(first, count):
        units = pl.ds(first, count)
        g = lax.dot_general(tokens[...], w_gate[units, :], NT, preferred_element_type=f32)
        u = lax.dot_general(tokens[...], w_up[units, :], NT, preferred_element_type=f32)
        act[:, units] = (silu(g) * u).astype(bf16)

    chunk = min(256, ff_total)

    def units_step(i, carry):
        hidden_units(pl.multiple_of(i * chunk, chunk), chunk)
        return carry

    lax.fori_loop(0, ff_total // chunk, units_step, 0)
    if ff_total % chunk:
        hidden_units(ff_total // chunk * chunk, ff_total % chunk)

    def down_step(q, carry):
        columns = pl.ds(pl.multiple_of(q * cols, cols), cols)
        spread_rows(q, dot(act[...], w_down[:, columns]))
        return carry

    lax.fori_loop(0, n_exp, down_step, 0)
    pack(back_out)
    exchange(back_out, back_in, 3)
    back_in[me_c] = back_out[me_c]
    wait_bytes(back_in, n_ctx - 1, ctx_recv.at[3])

    unpack(back_in)

    def moe_columns(q):
        value = jnp.concatenate([column_rows(s, q) for s in range(per_dev)], axis=0)
        return dot(gate_high, value) + dot(gate_low, value)

    for d in range(1, n_exp):
        peer = exp_peer(d)
        moe_out[peer] = moe_columns(peer).astype(bf16)
        to_exp(moe_out.at[peer], moe_in.at[me_e], exp_send.at[2], exp_recv.at[2], peer).start()
    total = moe_columns(me_e) + hidden[me_e].astype(f32)
    wait_bytes(moe_in, n_exp - 1, exp_recv.at[2])
    for d in range(1, n_exp):
        total = total + moe_in[exp_peer(d)].astype(f32)
    out_ref[...] = total.astype(bf16)

    wait_bytes(state_out, n_ctx - 1, ctx_send.at[0])
    wait_bytes(enter_out, n_ctx - 1, ctx_send.at[1])
    wait_bytes(rows_out, n_ctx - 1, ctx_send.at[2])
    wait_bytes(back_out, n_ctx - 1, ctx_send.at[3])
    for phase in range(3):
        wait_bytes(mix_out, n_exp - 1, exp_send.at[phase])
    for group, slots in enumerate((6, 3, 3, 6, 3)):
        wait_bytes(w_gate, slots * ff_part, w_send.at[group])


def per_device(n_ctx, n_exp, *args):
    (x, z, b, c, step, rate, norm_gain, out_w, stream, moe_gain, router, ids, wg, wu, wd) = args
    t, width = x.shape
    cols = stream.shape[1]
    d_model = cols * n_exp
    ff_part = wg.shape[1]
    ff_total = ff_part * n_exp
    part_rows = width // n_ctx
    stride = SLOTS // n_exp * n_exp
    row_count = n_ctx * (SLOTS // n_exp)
    vmem, dma = pltpu.VMEM, pltpu.SemaphoreType.DMA
    in_vmem = pl.BlockSpec(memory_space=pltpu.VMEM)
    anywhere = pl.BlockSpec(memory_space=pl.ANY)
    specs = [in_vmem] * 7 + [anywhere] + [in_vmem] * 4 + [anywhere] * 3
    return pl.pallas_call(
        functools.partial(layer_kernel, n_ctx, n_exp),
        out_shape=jax.ShapeDtypeStruct((t, cols), bf16),
        in_specs=specs,
        out_specs=in_vmem,
        scratch_shapes=[
            vmem(out_w.shape, bf16),
            vmem((ff_total, d_model), bf16),
            vmem((ff_total, d_model), bf16),
            vmem((ff_total, d_model), bf16),
            vmem((n_ctx, 2 * part_rows + 8, N), bf16),
            vmem((n_ctx, 2 * part_rows + 8, N), bf16),
            vmem((n_ctx, part_rows, N), f32),
            vmem((n_ctx, part_rows, N), f32),
            vmem((t, width), f32),
            vmem((t, width), bf16),
            vmem((n_exp, t, cols), bf16),
            vmem((n_exp, t, cols), bf16),
            vmem((n_exp, t, cols), bf16),
            vmem((t, d_model), bf16),
            vmem((cols // LANES, n_ctx * stride, LANES), f32),
            vmem((n_ctx, stride, cols), bf16),
            vmem((n_ctx, stride, cols), bf16),
            vmem((row_count, d_model), bf16),
            vmem((row_count, ff_total), bf16),
            vmem((n_ctx, stride, cols), bf16),
            vmem((n_ctx, stride, cols), bf16),
            vmem((n_exp, t, cols), bf16),
            vmem((n_exp, t, cols), bf16),
            dma((4,)),
            dma((4,)),
            dma((4,)),
            dma((3,)),
            dma((3,)),
            dma((5,)),
            dma((6,)),
        ],
        compiler_params=pltpu.CompilerParams(
            collective_id=0, has_side_effects=True, vmem_limit_bytes=56 * 1024 * 1024
        ),
        name="layer",
    )(
        x,
        z,
        b,
        c,
        step,
        rate.reshape(-1, 1),
        norm_gain.reshape(1, -1),
        out_w,
        stream,
        moe_gain.reshape(1, -1),
        router,
        ids,
        wg[0],
        wu[0],
        wd[0],
    )


def solution(mesh):
    in_specs = (
        P("ctx", "exp"),
        P("ctx", "exp"),
        P("ctx", "exp"),
        P("ctx", "exp"),
        P("exp", "ctx"),
        P("exp"),
        P("exp"),
        P("exp", None),
        P("ctx", "exp"),
        P(),
        P(),
        P("ctx", None),
        P("ctx", "exp", None),
        P("ctx", "exp", None),
        P("ctx", "exp", None),
    )
    return jax.shard_map(
        functools.partial(per_device, mesh.shape["ctx"], mesh.shape["exp"]),
        mesh=mesh,
        in_specs=in_specs,
        out_specs=P("ctx", "exp"),
        check_vma=False,
    )
```

time: 860 us -> 163 us (0.19)
  waiting for transfers between devices: 473 us -> 0 us
  blocking collectives: 269 us -> 0 us
  Pallas kernels: 0 us -> 156 us
  local copies, waits for them, and re-layouts: 60.4 us -> 6.16 us
  matrix products: 15.6 us -> 0 us
  between operations: 13.4 us -> 0.01 us
  starting transfers between devices: 13.2 us -> 0 us
  other arithmetic: 12.5 us -> 0 us
    all_to_all x1 -> x0, blocking collectives: 196 us -> none  [per_device(): lax.all_to_all(outgoing, 'ctx', split_axis=0, concat_axis=0, tiled=True)]
    all_to_all x1 -> x0, waiting for transfers between devices: 180 us -> none  [run_rows(): lax.all_to_all(shaped, 'ctx', split_axis=0, concat_axis=0, tiled=True)]
    pallas_call x0 -> x1, Pallas kernels: none -> 156 us  [per_device(): pl.pallas_call(functools.partial(layer_kernel, n_ctx, n_exp), out_shape=j...]
    psum x1 -> x0, waiting for transfers between devices: 135 us -> none  [per_device(): hidden_all = lax.psum(with_stream.astype(jnp.bfloat16), 'exp')]
    all_gather x1 -> x0, waiting for transfers between devices: 118 us -> none  [entering_2(): gathered = jax.tree.map(lambda a: lax.all_gather(a, axis), part)]
    all_gather x1 -> x0, blocking collectives: 72.3 us -> none  [entering_2(): gathered = jax.tree.map(lambda a: lax.all_gather(a, axis), part)]
    reduce_scatter x1 -> x0, waiting for transfers between devices: 39.8 us -> none  [per_device(): lax.psum_scatter(moe_part.astype(jnp.bfloat16), 'exp', scatter_dimension=...]
    gather x7 -> x0, local copies, waits for them, and re-layouts: 33.5 us -> none  [the longest x6 27.6 us: per_device(): picked_rows = flat_back[slot_rows[:, choice_number]].astype(jnp.float32)]
  transfers between devices with their start and end apart: 4 -> 0, of which waited for: 4 -> 0; matrix products, arithmetic and copies ran while one was open for 1% -> 0% of each run, Pallas kernels for 0% -> 0%
where the time goes in v1:
time: 163 us
  Pallas kernels  156 us (96%)
  local copies, waits for them, and re-layouts  6.16 us (4%)
    pallas_call x1, Pallas kernels, per_device(): pl.pallas_call(functools.partial(layer_kernel, n_ctx, n_exp), out_shape=j...  156 us
    unnamed x3, local copies, waits for them, and re-layouts  4.84 us

profile of v1, /device:TPU:1, one launch (start us, length us, event | category | flops | bytes accessed | tf_op | source)
XLA Modules:
  0.0 162.6 jit_solution(5864320950632190490)
XLA Ops:
  0.0 1.3 copy.16.rate_ref
  1.3 1.4 copy.18.ids_ref
  2.7 1.9 %copy.17.router_ref = bf16[2048,64]{1,0:T(8,128)(2,1)} copy(bf16[2048,64]{0,1:T(8,128)(2,1)} %param.25) | data formatting | bytes 524288 | tf_op args[10]
  4.7 156.4 %layer.1 = bf16[128,256]{1,0:T(8,128)(2,1)} custom-call(bf16[128,512]{1,0:T(8,128)(2,1)} %x_ref.1, bf16[128,512]{1,0:T(8,128)(2,1)} %z_ref.1, bf16[128,128]{1,0:T(8,128)(2,1)} %b_ref.1, bf16[128,128]{1,0:T(8,128)(2,1)} %c_ref.1, f32[8,128]{1,0:T(8,128)} %step_ref.1, f32[8,1]{1,0:T(8,128)} %copy.16.rate_ref, f32[1,512]{1,0:T(1,128)} %bitcast.10, ...), custom_call_target="tpu_custom_call" | custom-call | tf_op jit(solution)/shard_map/layer/pallas_call | solution.py:464
  161.1 1.5 copy.20

commit v2 on v1

--- a/solution.py
+++ b/solution.py
@@ -43,6 +43,22 @@
 def layer_kernel(
     n_ctx,
     n_exp,
+    x_hbm,
+    z_hbm,
+    b_hbm,
+    c_hbm,
+    step_hbm,
+    rate_hbm,
+    norm_gain_hbm,
+    out_w_hbm,
+    stream_hbm,
+    moe_gain_hbm,
+    router_hbm,
+    ids_hbm,
+    w_gate_hbm,
+    w_up_hbm,
+    w_down_hbm,
+    out_ref,
     x_ref,
     z_ref,
     b_ref,
@@ -50,16 +66,11 @@
     step_ref,
     rate_ref,
     norm_gain_ref,
-    out_w_hbm,
+    out_w,
     stream_ref,
     moe_gain_ref,
     router_ref,
     ids_ref,
-    w_gate_hbm,
-    w_up_hbm,
-    w_down_hbm,
-    out_ref,
-    out_w,
     w_gate,
     w_up,
     w_down,
@@ -104,7 +115,10 @@
     stride = per_dev * n_exp
 
     def ctx_peer(d):
-        return lax.rem(me_c + d, n_ctx)
+        odd, away = lax.rem(d, 2), (d + 1) // 2
+        return lax.rem(me_c + odd * away + (1 - odd) * (n_ctx - away), n_ctx)
+
+    far_first = sorted(range(1, n_exp), key=lambda d: (abs(d - n_exp // 2), d))
 
     def exp_peer(d):
         return lax.rem(me_e + d, n_exp)
@@ -147,23 +161,46 @@
     lax.fori_loop(1, n_ctx, greet_ctx, 0)
     lax.fori_loop(1, n_exp, greet_exp, 0)
 
-    out_w_copy = pltpu.make_async_copy(out_w_hbm, out_w, local_sem.at[0])
-    out_w_copy.start()
+    fetched = [
+        pltpu.make_async_copy(hbm, vmem, local_sem.at[3 + i])
+        for i, (hbm, vmem) in enumerate(
+            (
+                (step_hbm, step_ref),
+                (rate_hbm, rate_ref),
+                (x_hbm, x_ref),
+                (b_hbm, b_ref),
+                (c_hbm, c_ref),
+                (z_hbm, z_ref),
+                (ids_hbm, ids_ref),
+                (norm_gain_hbm, norm_gain_ref),
+                (stream_hbm, stream_ref),
+                (moe_gain_hbm, moe_gain_ref),
+                (router_hbm, router_ref),
+                (out_w_hbm, out_w),
+            )
+        )
+    ]
+    for copy in fetched:
+        copy.start()
     weights = ((w_gate_hbm, w_gate), (w_up_hbm, w_up), (w_down_hbm, w_down))
 
     def part(ref, index, first=0, rows=ff_part):
         return ref.at[pl.ds(pl.multiple_of(index * ff_part + first, 16), rows)]
 
     own_copies = [
-        pltpu.make_async_copy(hbm, part(buf, me_e), local_sem.at[1 + i])
+        pltpu.make_async_copy(hbm, part(buf, me_e), local_sem.at[i])
         for i, (hbm, buf) in enumerate(weights)
     ]
     for copy in own_copies:
         copy.start()
 
+    for copy in fetched[0:4]:
+        copy.wait()
     step = step_ref[...]
+    diagonal = iota((head_count, head_count), 0) == iota((head_count, head_count), 1)
+    rate = jnp.sum(jnp.where(diagonal, rate_ref[...], 0.0), axis=1, keepdims=True)
     lane_t = iota((head_count, token_count), 1)
-    running = -(step * rate_ref[...])
+    running = -(step * rate)
     shift = 1
     while shift < token_count:
         running = running + jnp.where(lane_t >= shift, pltpu.roll(running, shift, 1), 0.0)
@@ -186,23 +223,14 @@
             first_half, per_head[:, 2 * k : 2 * k + 1], per_head[:, 2 * k + 1 : 2 * k + 2]
         )
 
-    b_block, c_block = b_ref[...], c_ref[...]
-    scores = lax.dot_general(c_block, b_block, NT, preferred_element_type=f32)
-    lower = iota((token_count, token_count), 0) >= iota((token_count, token_count), 1)
-
-    def mix_head(h, weighted):
-        spread = run_t[:, h : h + 1] - running[h : h + 1, :]
-        decay = jnp.where(lower, jnp.exp(jnp.where(lower, spread, 0.0)), 0.0)
-        return dot((decay * scores).astype(bf16), weighted)
-
+    b_block = b_ref[...]
     row8 = iota((8, N), 0)
+    weighted = []
     for k in range(pair_count):
         lanes = slice(k * LANES, (k + 1) * LANES)
-        weighted = (expand(step_t, k) * x_ref[:, lanes].astype(f32)).astype(bf16)
-        inner[:, lanes] = jnp.where(
-            first_half, mix_head(2 * k, weighted), mix_head(2 * k + 1, weighted)
-        )
-        carried = (expand(tail, k) * weighted.astype(f32)).T.astype(bf16)
+        stepped = (expand(step_t, k) * x_ref[:, lanes].astype(f32)).astype(bf16)
+        weighted.append(stepped)
+        carried = (expand(tail, k) * stepped.astype(f32)).T.astype(bf16)
         state = dot(carried, b_block)
         for i in range(LANES // part_rows):
             j = k * LANES // part_rows + i
@@ -232,35 +260,60 @@
     sibling = me_x * CORES + 1 - core
     half = ff_part // 32 * 16
 
-    def send_part(buf, index, first, rows, group, arrival, peer, hbm=None):
+    def send_part(i, index, first, rows, group, arrival, peer, hbm=None):
+        buf = weights[i][1]
         to_exp(
             part(buf, index, first, rows) if hbm is None else hbm,
             part(buf, index, first, rows),
-            w_send.at[group],
-            w_recv.at[arrival],
+            w_send.at[i, group],
+            w_recv.at[i, arrival],
             peer,
         ).start()
 
-    for hbm, buf in weights:
-        send_part(buf, me_e, 0, ff_part, 0, 0, right, hbm)
-        send_part(buf, me_e, 0, ff_part, 0, 1, left, hbm)
-    for hbm, buf in weights:
-        send_part(buf, me_e, 0, ff_part, 1, 3, sibling, hbm)
-
-    def pass_on_neighbours():
-        wait_bytes(w_gate, 3 * ff_part, w_recv.at[0])
-        wait_bytes(w_gate, 3 * ff_part, w_recv.at[1])
-        for _, buf in weights:
-            send_part(buf, left, 0, half, 2, 2, right)
-            send_part(buf, right, half, ff_part - half, 2, 2, left)
-        for _, buf in weights:
-            send_part(buf, left, 0, ff_part, 3, 4, sibling)
-            send_part(buf, right, 0, ff_part, 3, 4, sibling)
-
-    def pass_on_opposite():
-        wait_bytes(w_gate, 3 * ff_part, w_recv.at[2])
-        for _, buf in weights:
-            send_part(buf, opposite, 0, ff_part, 4, 5, sibling)
+    def arrived(i, arrival, slots):
+        wait_bytes(w_gate, slots * ff_part, w_recv.at[i, arrival])
+
+    def send_own(i):
+        hbm = weights[i][0]
+        send_part(i, me_e, 0, ff_part, 0, 0, right, hbm)
+        send_part(i, me_e, 0, ff_part, 0, 1, left, hbm)
+        send_part(i, me_e, 0, ff_part, 1, 3, sibling, hbm)
+
+    def pass_on_neighbours(i):
+        arrived(i, 0, 1)
+        arrived(i, 1, 1)
+        send_part(i, left, 0, half, 2, 2, right)
+        send_part(i, right, half, ff_part - half, 2, 2, left)
+        send_part(i, left, 0, ff_part, 3, 4, sibling)
+        send_part(i, right, 0, ff_part, 3, 4, sibling)
+
+    def pass_on_opposite(i):
+        arrived(i, 2, 1)
+        send_part(i, opposite, 0, ff_part, 4, 5, sibling)
+
+    def complete(i):
+        own_copies[i].wait()
+        arrived(i, 3, 1)
+        arrived(i, 4, 2)
+        arrived(i, 5, 1)
+
+    send_own(0)
+    send_own(1)
+
+    fetched[4].wait()
+    c_block = c_ref[...]
+    scores = lax.dot_general(c_block, b_block, NT, preferred_element_type=f32)
+    lower = iota((token_count, token_count), 0) >= iota((token_count, token_count), 1)
+
+    def mix_head(h, values):
+        spread = run_t[:, h : h + 1] - running[h : h + 1, :]
+        decay = jnp.where(lower, jnp.exp(jnp.where(lower, spread, 0.0)), 0.0)
+        return dot((decay * scores).astype(bf16), values)
+
+    for k in range(pair_count):
+        inner[:, k * LANES : (k + 1) * LANES] = jnp.where(
+            first_half, mix_head(2 * k, weighted[k]), mix_head(2 * k + 1, weighted[k])
+        )
 
     state_in[me_c] = state_out[me_c]
     wait_bytes(state_in, n_ctx - 1, ctx_recv.at[0])
@@ -273,20 +326,23 @@
         decay = terms[0:1] + terms[1:2] + terms[2:3]
         return decay * entering + (block[0:r] + block[r : 2 * r])
 
-    lax.fori_loop(0, n_ctx, chain, jnp.zeros((part_rows, N), f32))
+    lax.fori_loop(0, n_ctx, chain, jnp.zeros((part_rows, N), f32), unroll=min(8, n_ctx))
     exchange(enter_out, enter_in, 1)
     enter_in[me_c] = enter_out[me_c]
-
-    lane_r = iota((token_count, row_count), 1)
-    expert_of, slot_of = lax.rem(lane_r, n_ctx), lane_r // n_ctx
-    named = jnp.zeros((token_count, row_count), f32)
-    for k in range(ids_ref.shape[1]):
-        named = named + jnp.where(ids_ref[:, k : k + 1] == expert_of, 1.0, 0.0)
-    strictly = iota((token_count, token_count), 0) > iota((token_count, token_count), 1)
-    rank = dot(jnp.where(strictly, 1.0, 0.0).astype(bf16), named.astype(bf16))
+    pass_on_neighbours(0)
+
+    for copy in fetched[5:]:
+        copy.wait()
+    row_r = iota((row_count, token_count), 0)
+    expert_of, slot_of = lax.rem(row_r, n_ctx), row_r // n_ctx
+    named = jnp.zeros((row_count, token_count), f32)
+    for k in range(ids_ref.shape[0]):
+        named = named + jnp.where(ids_ref[k : k + 1, :] == expert_of, 1.0, 0.0)
+    earlier = iota((token_count, token_count), 0) < iota((token_count, token_count), 1)
+    rank = dot(named.astype(bf16), jnp.where(earlier, 1.0, 0.0).astype(bf16))
     wanted = (slot_of + me_e * per_dev).astype(f32)
     chosen = jnp.where(rank == wanted, named, 0.0)
-    rows_of = chosen.T.astype(bf16)
+    rows_of = chosen.astype(bf16)
     gating = [silu(z_ref[:, k * LANES : (k + 1) * LANES].astype(f32)) for k in range(pair_count)]
 
     wait_bytes(enter_in, n_ctx - 1, ctx_recv.at[1])
@@ -310,12 +366,10 @@
         lanes = slice(k * LANES, (k + 1) * LANES)
         mixed[:, lanes] = (gated[k] * inverse * norm_gain_ref[:, lanes]).astype(bf16)
 
-    out_w_copy.wait()
-
     def out_columns(q):
         return dot(mixed[...], out_w[:, pl.ds(pl.multiple_of(q * cols, cols), cols)])
 
-    for d in range(1, n_exp):
+    for d in far_first:
         peer = exp_peer(d)
         mix_out[peer] = out_columns(peer).astype(bf16)
         to_exp(mix_out.at[peer], mix_in.at[me_e], exp_send.at[0], exp_recv.at[0], peer).start()
@@ -324,7 +378,7 @@
     for d in range(1, n_exp):
         own = own + mix_in[exp_peer(d)].astype(f32)
     hidden[me_e] = own.astype(bf16)
-    for d in range(1, n_exp):
+    for d in far_first:
         to_exp(
             hidden.at[me_e], hidden.at[me_e], exp_send.at[1], exp_recv.at[1], exp_peer(d)
         ).start()
@@ -356,6 +410,9 @@
             axis=1,
         ).astype(bf16)
 
+    send_own(2)
+    pass_on_neighbours(1)
+    pass_on_opposite(0)
     squares = jnp.zeros((token_count, cols), f32)
     for q in range(n_exp):
         h = hidden[q].astype(f32)
@@ -369,17 +426,18 @@
     pack(rows_out)
     exchange(rows_out, rows_in, 2)
     rows_in[me_c] = rows_out[me_c]
-    pass_on_neighbours()
-
-    logits = dot(expert_in[...], router_ref[...])
+
+    logits = lax.dot_general(expert_in[...], router_ref[...], NT, preferred_element_type=f32)
+    named_t, chosen_t = named.T, chosen.T
     score = 1.0 / (1.0 + jnp.exp(-logits))
-    picked_score = score * named[:, 0:n_ctx]
+    picked_score = score * named_t[:, 0:n_ctx]
     gate = picked_score / jnp.sum(picked_score, axis=1, keepdims=True)
-    gate_rows = jnp.concatenate([gate] * per_dev, axis=1) * chosen
+    gate_rows = jnp.concatenate([gate] * per_dev, axis=1) * chosen_t
     gate_lead = leading(gate_rows)
     gate_high = gate_lead.astype(bf16)
     gate_low = (gate_rows - gate_lead).astype(bf16)
-    pass_on_opposite()
+    pass_on_neighbours(2)
+    pass_on_opposite(1)
 
     wait_bytes(rows_in, n_ctx - 1, ctx_recv.at[2])
 
@@ -388,11 +446,9 @@
         for s in range(per_dev):
             tokens[s * n_ctx : (s + 1) * n_ctx, q * cols : (q + 1) * cols] = column_rows(s, q)
 
-    for copy in own_copies:
-        copy.wait()
-    wait_bytes(w_gate, 3 * ff_part, w_recv.at[3])
-    wait_bytes(w_gate, 6 * ff_part, w_recv.at[4])
-    wait_bytes(w_gate, 3 * ff_part, w_recv.at[5])
+    complete(0)
+    complete(1)
+    pass_on_opposite(2)
 
     def hidden_units(first, count):
         units = pl.ds(first, count)
@@ -410,6 +466,8 @@
     if ff_total % chunk:
         hidden_units(ff_total // chunk * chunk, ff_total % chunk)
 
+    complete(2)
+
     def down_step(q, carry):
         columns = pl.ds(pl.multiple_of(q * cols, cols), cols)
         spread_rows(q, dot(act[...], w_down[:, columns]))
@@ -427,7 +485,7 @@
         value = jnp.concatenate([column_rows(s, q) for s in range(per_dev)], axis=0)
         return dot(gate_high, value) + dot(gate_low, value)
 
-    for d in range(1, n_exp):
+    for d in far_first:
         peer = exp_peer(d)
         moe_out[peer] = moe_columns(peer).astype(bf16)
         to_exp(moe_out.at[peer], moe_in.at[me_e], exp_send.at[2], exp_recv.at[2], peer).start()
@@ -443,8 +501,9 @@
     wait_bytes(back_out, n_ctx - 1, ctx_send.at[3])
     for phase in range(3):
         wait_bytes(mix_out, n_exp - 1, exp_send.at[phase])
-    for group, slots in enumerate((6, 3, 3, 6, 3)):
-        wait_bytes(w_gate, slots * ff_part, w_send.at[group])
+    for i in range(3):
+        for group, slots in enumerate((2, 1, 1, 2, 1)):
+            wait_bytes(w_gate, slots * ff_part, w_send.at[i, group])
 
 
 def per_device(n_ctx, n_exp, *args):
@@ -458,16 +517,17 @@
     stride = SLOTS // n_exp * n_exp
     row_count = n_ctx * (SLOTS // n_exp)
     vmem, dma = pltpu.VMEM, pltpu.SemaphoreType.DMA
-    in_vmem = pl.BlockSpec(memory_space=pltpu.VMEM)
     anywhere = pl.BlockSpec(memory_space=pl.ANY)
-    specs = [in_vmem] * 7 + [anywhere] + [in_vmem] * 4 + [anywhere] * 3
+    rate, norm_gain, moe_gain = (v.reshape(1, -1) for v in (rate, norm_gain, moe_gain))
+    router, ids = router.T, ids.T
+    inputs = (x, z, b, c, step, rate, norm_gain, out_w, stream, moe_gain, router, ids)
     return pl.pallas_call(
         functools.partial(layer_kernel, n_ctx, n_exp),
         out_shape=jax.ShapeDtypeStruct((t, cols), bf16),
-        in_specs=specs,
-        out_specs=in_vmem,
+        in_specs=[anywhere] * 15,
+        out_specs=pl.BlockSpec(memory_space=pltpu.VMEM),
         scratch_shapes=[
-            vmem(out_w.shape, bf16),
+            *(vmem(v.shape, v.dtype) for v in inputs),
             vmem((ff_total, d_model), bf16),
             vmem((ff_total, d_model), bf16),
             vmem((ff_total, d_model), bf16),
@@ -490,31 +550,20 @@
             vmem((n_ctx, stride, cols), bf16),
             vmem((n_exp, t, cols), bf16),
             vmem((n_exp, t, cols), bf16),
-            dma((4,)),
+            dma((15,)),
             dma((4,)),
             dma((4,)),
             dma((3,)),
             dma((3,)),
-            dma((5,)),
-            dma((6,)),
+            dma((3, 5)),
+            dma((3, 6)),
         ],
         compiler_params=pltpu.CompilerParams(
             collective_id=0, has_side_effects=True, vmem_limit_bytes=56 * 1024 * 1024
         ),
         name="layer",
     )(
-        x,
-        z,
-        b,
-        c,
-        step,
-        rate.reshape(-1, 1),
-        norm_gain.reshape(1, -1),
-        out_w,
-        stream,
-        moe_gain.reshape(1, -1),
-        router,
-        ids,
+        *inputs,
         wg[0],
         wu[0],
         wd[0],

time: 163 us -> 151 us (0.926)
  Pallas kernels: 156 us -> 149 us
  local copies, waits for them, and re-layouts: 6.16 us -> 1.47 us
    pallas_call x1, Pallas kernels: 156 us -> 149 us  [per_device(): pl.pallas_call(functools.partial(layer_kernel, n_ctx, n_exp), out_shape=j...]
    unnamed x3 -> x1, local copies, waits for them, and re-layouts: 4.84 us -> 1.47 us
where the time goes in v2:
time: 151 us
  Pallas kernels  149 us (99%)
    pallas_call x1, Pallas kernels, per_device(): pl.pallas_call(functools.partial(layer_kernel, n_ctx, n_exp), out_shape=j...  149 us

profile of v2, /device:TPU:1, one launch (start us, length us, event | category | flops | bytes accessed | tf_op | source)
XLA Modules:
  0.0 150.9 jit_solution(5102139214848669875)
XLA Ops:
  0.0 149.5 %layer.1 = bf16[128,256]{1,0:T(8,128)(2,1)} custom-call(bf16[128,512]{1,0:T(8,128)(2,1)} %x_hbm.1, bf16[128,512]{1,0:T(8,128)(2,1)} %z_hbm.1, bf16[128,128]{1,0:T(8,128)(2,1)} %b_hbm.1, bf16[128,128]{1,0:T(8,128)(2,1)} %c_hbm.1, f32[8,128]{1,0:T(8,128)} %step_hbm.1, f32[1,8]{1,0:T(1,128)} %bitcast.15, f32[1,512]{1,0:T(1,128)} %bitcast.14, ...), custom_call_target="tpu_custom_call" | custom-call | tf_op jit(solution)/shard_map/layer/pallas_call | solution.py:524
  149.5 1.5 copy.17

commit v3 on v2

--- a/solution.py
+++ b/solution.py
@@ -11,6 +11,7 @@
 N = 128
 LANES = 128
 SLOTS = 16
+PARTS = 2
 CORES = 2
 MESH = pl.DeviceIdType.MESH
 NT = (((1,), (1,)), ((), ()))
@@ -76,6 +77,8 @@
     w_down,
     state_out,
     state_in,
+    decay_out,
+    decay_in,
     enter_out,
     enter_in,
     inner,
@@ -98,6 +101,8 @@
     ctx_recv,
     exp_send,
     exp_recv,
+    pair_recv,
+    hidden_recv,
     w_send,
     w_recv,
 ):
@@ -112,13 +117,11 @@
     ff_total = ff_part * n_exp
     per_dev = SLOTS // n_exp
     row_count = n_ctx * per_dev
-    stride = per_dev * n_exp
 
     def ctx_peer(d):
         odd, away = lax.rem(d, 2), (d + 1) // 2
         return lax.rem(me_c + odd * away + (1 - odd) * (n_ctx - away), n_ctx)
 
-    far_first = sorted(range(1, n_exp), key=lambda d: (abs(d - n_exp // 2), d))
 
     def exp_peer(d):
         return lax.rem(me_e + d, n_exp)
@@ -133,11 +136,11 @@
             device_id_type=MESH,
         )
 
-    def exchange(src, dst, phase):
+    def exchange(src, dst, phase, entry=lambda peer: peer):
         def one(d, carry):
             peer = ctx_peer(d)
             pltpu.make_async_remote_copy(
-                src_ref=src.at[peer],
+                src_ref=src.at[entry(peer)],
                 dst_ref=dst.at[me_c],
                 send_sem=ctx_send.at[phase],
                 recv_sem=ctx_recv.at[phase],
@@ -146,7 +149,7 @@
             ).start()
             return carry
 
-        lax.fori_loop(1, n_ctx, one, 0)
+        lax.fori_loop(1, n_ctx, one, 0, unroll=3 if n_ctx % 3 == 1 else 1)
 
     barrier = pltpu.get_barrier_semaphore()
 
@@ -215,6 +218,8 @@
     tail = jnp.exp(last - run_t)
     grown = jnp.exp(run_t)
     total_decay = jnp.exp(last)
+    for h in range(head_count):
+        decay_out[h] = jnp.broadcast_to(total_decay[:, h : h + 1], (1, N))
 
     first_half = iota((token_count, LANES), 1) < P_SIZE
 
@@ -224,7 +229,6 @@
         )
 
     b_block = b_ref[...]
-    row8 = iota((8, N), 0)
     weighted = []
     for k in range(pair_count):
         lanes = slice(k * LANES, (k + 1) * LANES)
@@ -234,21 +238,14 @@
         state = dot(carried, b_block)
         for i in range(LANES // part_rows):
             j = k * LANES // part_rows + i
-            head = j * part_rows // P_SIZE
-            decay = jnp.broadcast_to(total_decay[:, head : head + 1], (8, N))
-            high = leading(decay)
-            middle = leading(decay - high)
-            low = decay - high - middle
-            decay_rows = jnp.where(
-                row8 == 0, high, jnp.where(row8 == 1, middle, jnp.where(row8 == 2, low, 0.0))
-            )
             piece = state[i * part_rows : (i + 1) * part_rows, :]
             lead = leading(piece)
-            state_out[j] = jnp.concatenate([lead, piece - lead, decay_rows], axis=0).astype(bf16)
+            state_out[j] = jnp.concatenate([lead, piece - lead], axis=0).astype(bf16)
 
     pl.semaphore_wait(barrier, n_ctx - 1 + n_exp - 1)
 
     exchange(state_out, state_in, 0)
+    exchange(decay_out, decay_in, 6, lambda peer: peer * part_rows // P_SIZE)
 
     chips = n_exp // CORES
     me_x, core = me_e // CORES, lax.rem(me_e, CORES)
@@ -316,20 +313,19 @@
         )
 
     state_in[me_c] = state_out[me_c]
+    decay_in[me_c] = decay_out[me_c * part_rows // P_SIZE]
     wait_bytes(state_in, n_ctx - 1, ctx_recv.at[0])
+    wait_bytes(decay_in, n_ctx - 1, ctx_recv.at[6])
 
     def chain(i, entering):
         enter_out[i] = entering
         block = state_in[i].astype(f32)
         r = part_rows
-        terms = block[2 * r : 2 * r + 8]
-        decay = terms[0:1] + terms[1:2] + terms[2:3]
-        return decay * entering + (block[0:r] + block[r : 2 * r])
+        return decay_in[i] * entering + (block[0:r] + block[r : 2 * r])
 
     lax.fori_loop(0, n_ctx, chain, jnp.zeros((part_rows, N), f32), unroll=min(8, n_ctx))
     exchange(enter_out, enter_in, 1)
     enter_in[me_c] = enter_out[me_c]
-    pass_on_neighbours(0)
 
     for copy in fetched[5:]:
         copy.wait()
@@ -344,6 +340,8 @@
     chosen = jnp.where(rank == wanted, named, 0.0)
     rows_of = chosen.astype(bf16)
     gating = [silu(z_ref[:, k * LANES : (k + 1) * LANES].astype(f32)) for k in range(pair_count)]
+
+    pass_on_neighbours(0)
 
     wait_bytes(enter_in, n_ctx - 1, ctx_recv.at[1])
     entering = enter_in[...].reshape(width, N)
@@ -369,46 +367,79 @@
     def out_columns(q):
         return dot(mixed[...], out_w[:, pl.ds(pl.multiple_of(q * cols, cols), cols)])
 
-    for d in far_first:
-        peer = exp_peer(d)
-        mix_out[peer] = out_columns(peer).astype(bf16)
-        to_exp(mix_out.at[peer], mix_in.at[me_e], exp_send.at[0], exp_recv.at[0], peer).start()
-    own = out_columns(me_e) + stream_ref[...].astype(f32)
-    wait_bytes(mix_in, n_exp - 1, exp_recv.at[0])
-    for d in range(1, n_exp):
-        own = own + mix_in[exp_peer(d)].astype(f32)
+    away = (2, 1, 3)
+    for r in (*away, 0):
+        chip = lax.rem(me_x + r, chips)
+        mix_out[r] = out_columns(chip * CORES + 1 - core).astype(bf16)
+        to_exp(mix_out.at[r], mix_in.at[r], exp_send.at[0], pair_recv.at[r], sibling).start()
+
+    def pair_columns(r):
+        value = out_columns(at_chip(r))
+        wait_bytes(mix_in, 1, pair_recv.at[r])
+        return value + mix_in[r].astype(f32)
+
+    for r in away:
+        mix_out[chips + r] = pair_columns(r).astype(bf16)
+        to_exp(
+            mix_out.at[chips + r],
+            mix_in.at[2 * chips - r],
+            exp_send.at[1],
+            exp_recv.at[0],
+            at_chip(r),
+        ).start()
+    own = pair_columns(0) + stream_ref[...].astype(f32)
+    wait_bytes(mix_in, chips - 1, exp_recv.at[0])
+    for r in away:
+        own = own + mix_in[chips + r].astype(f32)
+
     hidden[me_e] = own.astype(bf16)
-    for d in far_first:
-        to_exp(
-            hidden.at[me_e], hidden.at[me_e], exp_send.at[1], exp_recv.at[1], exp_peer(d)
-        ).start()
-    wait_bytes(mix_in, n_exp - 1, exp_recv.at[1])
+    mine = hidden.at[me_e]
+    for r in away:
+        to_exp(mine, mine, exp_send.at[3], hidden_recv.at[chips - r], at_chip(r)).start()
+    to_exp(mine, mine, exp_send.at[3], hidden_recv.at[0], sibling).start()
+    for r in (1, 3, 2):
+        wait_bytes(hidden, 1, hidden_recv.at[r])
+        block = hidden.at[at_chip(r)]
+        to_exp(block, block, exp_send.at[4], hidden_recv.at[chips], sibling).start()
+    wait_bytes(hidden, 1, hidden_recv.at[0])
+    wait_bytes(hidden, chips - 1, hidden_recv.at[chips])
 
     tiles = [slice(i * LANES, (i + 1) * LANES) for i in range(cols // LANES)]
-
-    def spread_rows(q, value):
+    per_part = n_exp // PARTS
+    packet = per_dev * per_part
+
+    def places(s, q_in_part):
+        return pl.ds(s * per_part + q_in_part, n_ctx, stride=packet)
+
+    def spread_rows(p, q_in_part, value):
         for s in range(per_dev):
             for i, lanes in enumerate(tiles):
-                rows_f32.at[i][pl.ds(s * n_exp + q, n_ctx, stride=stride), :] = value[
+                rows_f32.at[p * len(tiles) + i][places(s, q_in_part), :] = value[
                     s * n_ctx : (s + 1) * n_ctx, lanes
                 ]
 
-    def pack(ref):
+    def pack(ref, p):
         for i, lanes in enumerate(tiles):
-            ref[:, :, lanes] = rows_f32[i].reshape(n_ctx, stride, LANES).astype(bf16)
-
-    def unpack(ref):
+            value = rows_f32[p * len(tiles) + i].reshape(n_ctx, packet, LANES)
+            ref[p, :, :, lanes] = value.astype(bf16)
+
+    def unpack(ref, p):
         for i, lanes in enumerate(tiles):
-            rows_f32[i] = ref[:, :, lanes].astype(f32).reshape(n_ctx * stride, LANES)
-
-    def column_rows(s, q):
+            value = ref[p, :, :, lanes].astype(f32)
+            rows_f32[p * len(tiles) + i] = value.reshape(n_ctx * packet, LANES)
+
+    def column_rows(s, p, q_in_part):
         return jnp.concatenate(
             [
-                rows_f32.at[i][pl.ds(s * n_exp + q, n_ctx, stride=stride), :]
+                rows_f32.at[p * len(tiles) + i][places(s, q_in_part), :]
                 for i in range(len(tiles))
             ],
             axis=1,
         ).astype(bf16)
+
+    def exchange_part(src, dst, p, phase):
+        exchange(src.at[p], dst.at[p], phase + p)
+        dst[p, me_c] = src[p, me_c]
 
     send_own(2)
     pass_on_neighbours(1)
@@ -422,10 +453,11 @@
         columns = slice(q * cols, (q + 1) * cols)
         value = hidden[q].astype(f32) * inverse * moe_gain_ref[:, columns]
         expert_in[:, columns] = value.astype(bf16)
-        spread_rows(q, dot(rows_of, expert_in[:, columns]))
-    pack(rows_out)
-    exchange(rows_out, rows_in, 2)
-    rows_in[me_c] = rows_out[me_c]
+        p, q_in_part = q // per_part, q % per_part
+        spread_rows(p, q_in_part, dot(rows_of, expert_in[:, columns]))
+        if q_in_part == per_part - 1:
+            pack(rows_out, p)
+            exchange_part(rows_out, rows_in, p, 2)
 
     logits = lax.dot_general(expert_in[...], router_ref[...], NT, preferred_element_type=f32)
     named_t, chosen_t = named.T, chosen.T
@@ -439,16 +471,19 @@
     pass_on_neighbours(2)
     pass_on_opposite(1)
 
-    wait_bytes(rows_in, n_ctx - 1, ctx_recv.at[2])
-
-    unpack(rows_in)
-    for q in range(n_exp):
-        for s in range(per_dev):
-            tokens[s * n_ctx : (s + 1) * n_ctx, q * cols : (q + 1) * cols] = column_rows(s, q)
+
+    for p in range(PARTS):
+        wait_bytes(rows_in.at[p], n_ctx - 1, ctx_recv.at[2 + p])
+        unpack(rows_in, p)
+        for q_in_part in range(per_part):
+            first = (p * per_part + q_in_part) * cols
+            for s in range(per_dev):
+                tokens[s * n_ctx : (s + 1) * n_ctx, first : first + cols] = column_rows(
+                    s, p, q_in_part
+                )
 
     complete(0)
     complete(1)
-    pass_on_opposite(2)
 
     def hidden_units(first, count):
         units = pl.ds(first, count)
@@ -466,30 +501,42 @@
     if ff_total % chunk:
         hidden_units(ff_total // chunk * chunk, ff_total % chunk)
 
+    pass_on_opposite(2)
     complete(2)
 
-    def down_step(q, carry):
-        columns = pl.ds(pl.multiple_of(q * cols, cols), cols)
-        spread_rows(q, dot(act[...], w_down[:, columns]))
-        return carry
-
-    lax.fori_loop(0, n_exp, down_step, 0)
-    pack(back_out)
-    exchange(back_out, back_in, 3)
-    back_in[me_c] = back_out[me_c]
-    wait_bytes(back_in, n_ctx - 1, ctx_recv.at[3])
-
-    unpack(back_in)
-
-    def moe_columns(q):
-        value = jnp.concatenate([column_rows(s, q) for s in range(per_dev)], axis=0)
+    for p in range(PARTS):
+
+        def down_step(q_in_part, carry, p=p):
+            first = (p * per_part + q_in_part) * cols
+            columns = pl.ds(pl.multiple_of(first, cols), cols)
+            spread_rows(p, q_in_part, dot(act[...], w_down[:, columns]))
+            return carry
+
+        lax.fori_loop(0, per_part, down_step, 0)
+        pack(back_out, p)
+        exchange_part(back_out, back_in, p, 4)
+
+    def moe_columns(p, q_in_part):
+        value = jnp.concatenate([column_rows(s, p, q_in_part) for s in range(per_dev)], axis=0)
         return dot(gate_high, value) + dot(gate_low, value)
 
-    for d in far_first:
-        peer = exp_peer(d)
-        moe_out[peer] = moe_columns(peer).astype(bf16)
-        to_exp(moe_out.at[peer], moe_in.at[me_e], exp_send.at[2], exp_recv.at[2], peer).start()
-    total = moe_columns(me_e) + hidden[me_e].astype(f32)
+    own_part, own_q = me_e // per_part, lax.rem(me_e, per_part)
+    for p in range(PARTS):
+        wait_bytes(back_in.at[p], n_ctx - 1, ctx_recv.at[4 + p])
+        unpack(back_in, p)
+        for away in range(per_part - 1, -1, -1):
+            q_in_part = lax.rem(own_q + away, per_part)
+            q = p * per_part + q_in_part
+
+            def send_columns(q=q, p=p, q_in_part=q_in_part):
+                moe_out[q] = moe_columns(p, q_in_part).astype(bf16)
+                to_exp(moe_out.at[q], moe_in.at[me_e], exp_send.at[2], exp_recv.at[2], q).start()
+
+            if away:
+                send_columns()
+            else:
+                pl.when(own_part != p)(send_columns)
+    total = moe_columns(own_part, own_q) + hidden[me_e].astype(f32)
     wait_bytes(moe_in, n_exp - 1, exp_recv.at[2])
     for d in range(1, n_exp):
         total = total + moe_in[exp_peer(d)].astype(f32)
@@ -497,10 +544,12 @@
 
     wait_bytes(state_out, n_ctx - 1, ctx_send.at[0])
     wait_bytes(enter_out, n_ctx - 1, ctx_send.at[1])
-    wait_bytes(rows_out, n_ctx - 1, ctx_send.at[2])
-    wait_bytes(back_out, n_ctx - 1, ctx_send.at[3])
-    for phase in range(3):
-        wait_bytes(mix_out, n_exp - 1, exp_send.at[phase])
+    wait_bytes(decay_in, n_ctx - 1, ctx_send.at[6])
+    for p in range(PARTS):
+        wait_bytes(rows_out.at[p], n_ctx - 1, ctx_send.at[2 + p])
+        wait_bytes(back_out.at[p], n_ctx - 1, ctx_send.at[4 + p])
+    for phase, count in enumerate((chips, chips - 1, n_exp - 1, chips, chips - 1)):
+        wait_bytes(mix_out, count, exp_send.at[phase])
     for i in range(3):
         for group, slots in enumerate((2, 1, 1, 2, 1)):
             wait_bytes(w_gate, slots * ff_part, w_send.at[i, group])
@@ -531,8 +580,10 @@
             vmem((ff_total, d_model), bf16),
             vmem((ff_total, d_model), bf16),
             vmem((ff_total, d_model), bf16),
-            vmem((n_ctx, 2 * part_rows + 8, N), bf16),
-            vmem((n_ctx, 2 * part_rows + 8, N), bf16),
+            vmem((n_ctx, 2 * part_rows, N), bf16),
+            vmem((n_ctx, 2 * part_rows, N), bf16),
+            vmem((step.shape[0], 1, N), f32),
+            vmem((n_ctx, 1, N), f32),
             vmem((n_ctx, part_rows, N), f32),
             vmem((n_ctx, part_rows, N), f32),
             vmem((t, width), f32),
@@ -541,20 +592,22 @@
             vmem((n_exp, t, cols), bf16),
             vmem((n_exp, t, cols), bf16),
             vmem((t, d_model), bf16),
-            vmem((cols // LANES, n_ctx * stride, LANES), f32),
-            vmem((n_ctx, stride, cols), bf16),
-            vmem((n_ctx, stride, cols), bf16),
+            vmem((PARTS * cols // LANES, n_ctx * stride // PARTS, LANES), f32),
+            vmem((PARTS, n_ctx, stride // PARTS, cols), bf16),
+            vmem((PARTS, n_ctx, stride // PARTS, cols), bf16),
             vmem((row_count, d_model), bf16),
             vmem((row_count, ff_total), bf16),
-            vmem((n_ctx, stride, cols), bf16),
-            vmem((n_ctx, stride, cols), bf16),
+            vmem((PARTS, n_ctx, stride // PARTS, cols), bf16),
+            vmem((PARTS, n_ctx, stride // PARTS, cols), bf16),
             vmem((n_exp, t, cols), bf16),
             vmem((n_exp, t, cols), bf16),
             dma((15,)),
+            dma((7,)),
+            dma((7,)),
+            dma((5,)),
+            dma((3,)),
             dma((4,)),
-            dma((4,)),
-            dma((3,)),
-            dma((3,)),
+            dma((5,)),
             dma((3, 5)),
             dma((3, 6)),
         ],

time: 151 us -> 142 us (0.940)
  Pallas kernels: 149 us -> 139 us
    pallas_call x1, Pallas kernels: 149 us -> 139 us  [per_device(): pl.pallas_call(functools.partial(layer_kernel, n_ctx, n_exp), out_shape=j...]
where the time goes in v3:
time: 142 us; the launch traced here: 141 us
  Pallas kernels  139 us (98%)
  local copies, waits for them, and re-layouts  1.47 us (1%)
    pallas_call x1, Pallas kernels, per_device(): pl.pallas_call(functools.partial(layer_kernel, n_ctx, n_exp), out_shape=j...  139 us

profile of v3, /device:TPU:1, one launch (start us, length us, event | category | flops | bytes accessed | tf_op | source)
XLA Modules:
  0.0 140.8 jit_solution(775536751553646493)
XLA Ops:
  0.0 139.4 %layer.1 = bf16[128,256]{1,0:T(8,128)(2,1)} custom-call(bf16[128,512]{1,0:T(8,128)(2,1)} %x_hbm.1, bf16[128,512]{1,0:T(8,128)(2,1)} %z_hbm.1, bf16[128,128]{1,0:T(8,128)(2,1)} %b_hbm.1, bf16[128,128]{1,0:T(8,128)(2,1)} %c_hbm.1, f32[8,128]{1,0:T(8,128)} %step_hbm.1, f32[1,8]{1,0:T(1,128)} %bitcast.15, f32[1,512]{1,0:T(1,128)} %bitcast.14, ...), custom_call_target="tpu_custom_call" | custom-call | tf_op jit(solution)/shard_map/layer/pallas_call | solution.py:573
  139.4 1.5 %copy.17 = bf16[128,256]{1,0:T(8,128)(2,1)} copy(bf16[128,256]{1,0:T(8,128)(2,1)} %layer.1) | data formatting | bytes 131072

commit v4 on v3

--- a/solution.py
+++ b/solution.py
@@ -119,7 +119,8 @@
     row_count = n_ctx * per_dev
 
     def ctx_peer(d):
-        odd, away = lax.rem(d, 2), (d + 1) // 2
+        back = n_ctx - d
+        odd, away = lax.rem(back, 2), (back + 1) // 2
         return lax.rem(me_c + odd * away + (1 - odd) * (n_ctx - away), n_ctx)
 
 
@@ -149,7 +150,7 @@
             ).start()
             return carry
 
-        lax.fori_loop(1, n_ctx, one, 0, unroll=3 if n_ctx % 3 == 1 else 1)
+        lax.fori_loop(1, n_ctx, one, 0, unroll=9 if n_ctx % 9 == 1 else 1)
 
     barrier = pltpu.get_barrier_semaphore()
 

time: 142 us -> 141 us (level)
  Pallas kernels: 139 us -> 137 us
    pallas_call x1, Pallas kernels: 139 us -> 137 us  [per_device(): pl.pallas_call(functools.partial(layer_kernel, n_ctx, n_exp), out_shape=j...]
where the time goes in v4:
time: 141 us; the launch traced here: 139 us
  Pallas kernels  137 us (97%)
  local copies, waits for them, and re-layouts  1.47 us (1%)
    pallas_call x1, Pallas kernels, per_device(): pl.pallas_call(functools.partial(layer_kernel, n_ctx, n_exp), out_shape=j...  137 us

profile of v4, /device:TPU:1, one launch (start us, length us, event | category | flops | bytes accessed | tf_op | source)
XLA Modules:
  0.0 138.7 jit_solution(17227918734985906223)
XLA Ops:
  0.0 137.2 %layer.1 = bf16[128,256]{1,0:T(8,128)(2,1)} custom-call(bf16[128,512]{1,0:T(8,128)(2,1)} %x_hbm.1, bf16[128,512]{1,0:T(8,128)(2,1)} %z_hbm.1, bf16[128,128]{1,0:T(8,128)(2,1)} %b_hbm.1, bf16[128,128]{1,0:T(8,128)(2,1)} %c_hbm.1, f32[8,128]{1,0:T(8,128)} %step_hbm.1, f32[1,8]{1,0:T(1,128)} %bitcast.15, f32[1,512]{1,0:T(1,128)} %bitcast.14, ...), custom_call_target="tpu_custom_call" | custom-call | tf_op jit(solution)/shard_map/layer/pallas_call | solution.py:574
  137.2 1.5 %copy.17 = bf16[128,256]{1,0:T(8,128)(2,1)} copy(bf16[128,256]{1,0:T(8,128)(2,1)} %layer.1) | data formatting | bytes 131072

commit v5 on v4

--- a/solution.py
+++ b/solution.py
@@ -498,11 +498,13 @@
         hidden_units(pl.multiple_of(i * chunk, chunk), chunk)
         return carry
 
-    lax.fori_loop(0, ff_total // chunk, units_step, 0)
+    early = ff_total // chunk * 3 // 5
+    lax.fori_loop(0, early, units_step, 0)
+    pass_on_opposite(2)
+    lax.fori_loop(early, ff_total // chunk, units_step, 0)
     if ff_total % chunk:
         hidden_units(ff_total // chunk * chunk, ff_total % chunk)
 
-    pass_on_opposite(2)
     complete(2)
 
     for p in range(PARTS):

time: 141 us -> 142 us (level); the launches traced: 139 us -> 142 us
  Pallas kernels: 137 us -> 141 us
    pallas_call x1, Pallas kernels: 137 us -> 141 us  [per_device(): pl.pallas_call(functools.partial(layer_kernel, n_ctx, n_exp), out_shape=j...]
where the time goes in v5:
time: 142 us
  Pallas kernels  141 us (99%)
  local copies, waits for them, and re-layouts  1.47 us (1%)
    pallas_call x1, Pallas kernels, per_device(): pl.pallas_call(functools.partial(layer_kernel, n_ctx, n_exp), out_shape=j...  141 us

profile of v5, /device:TPU:1, one launch (start us, length us, event | category | flops | bytes accessed | tf_op | source)
XLA Modules:
  0.0 142.2 jit_solution(4829568574894388862)
XLA Ops:
  0.0 140.7 %layer.1 = bf16[128,256]{1,0:T(8,128)(2,1)} custom-call(bf16[128,512]{1,0:T(8,128)(2,1)} %x_hbm.1, bf16[128,512]{1,0:T(8,128)(2,1)} %z_hbm.1, bf16[128,128]{1,0:T(8,128)(2,1)} %b_hbm.1, bf16[128,128]{1,0:T(8,128)(2,1)} %c_hbm.1, f32[8,128]{1,0:T(8,128)} %step_hbm.1, f32[1,8]{1,0:T(1,128)} %bitcast.15, f32[1,512]{1,0:T(1,128)} %bitcast.14, ...), custom_call_target="tpu_custom_call" | custom-call | tf_op jit(solution)/shard_map/layer/pallas_call | solution.py:576
  140.7 1.5 %copy.17 = bf16[128,256]{1,0:T(8,128)(2,1)} copy(bf16[128,256]{1,0:T(8,128)(2,1)} %layer.1) | data formatting | bytes 131072
